TPU v7x, 256 devices: a whole 4x4x8 slice. The times are simulated.
256 devices in a mesh: dp: 64 (over y, z, core), tensor: 4 (over x).
Axes of the slice: x: 4, y: 4, z: 8, core: 2. Of those that a mesh axis runs over, the one named last changes fastest.
Arguments:
- activations: bfloat16 [32768, 8192], P('dp', 'tensor'), may hold values from -2000 to 2000
- norm_gain: float32 [8192], replicated, may hold values from 0.5 to 12
- w_query: bfloat16 [8192, 4096], P('dp', 'tensor'), may hold values from -0.0625 to 0.0625
- w_key: bfloat16 [8192, 512], P('dp', 'tensor'), may hold values from -0.0625 to 0.0625
- w_value: bfloat16 [8192, 512], P('dp', 'tensor'), may hold values from -0.0625 to 0.0625
- lengths: int32 [128], replicated, may hold values from 128 to 256
- languages: int32 [128], replicated, may hold values from 0 to 29
- lang_caps: int32 [30], replicated, may hold values from 128 to 256
- dest_shard: int32 [128], replicated, may hold values from 0 to 63, as said below
Outputs:
- attended: bfloat16 [32768, 4096], P('dp', 'tensor')
Inputs may be any that keep to these rules, and one draw needn't show every extreme that they name: `dest_shard`: every data shard receives exactly 2 documents.
All inputs are finite; a program needn't handle non-finite values.
Results may differ from a plain program's by a relative error of at most 0.007.
The roundings to bfloat16 on the way count: a program that leaves them out, or rounds other values in their place, can miss the bound.
Values may be sent and summed in bfloat16 or wider, within the bound.
A program may use at most 128 MiB of HBM per device.

v0:
```python
import math
import jax
import jax.numpy as jnp
from jax import lax
from jax.sharding import PartitionSpec as P

HEAD_WIDTH = 128
rope_base = 500000.0
norm_eps = 1e-05


def rotary_embedding(vectors, token_positions):
    half_width = vectors.shape[-1] // 2
    steps_range = jnp.arange(half_width, dtype=jnp.float32)
    frequency = jnp.exp(steps_range * (-2.0 * math.log(rope_base) / vectors.shape[-1]))
    angles = token_positions[..., None, None] * frequency
    cosine = jnp.cos(angles)
    sine_table = jnp.sin(angles)
    first_half = vectors[..., :half_width]
    second_half = vectors[..., half_width:]
    return jnp.concatenate(
        [
            first_half * cosine - second_half * sine_table,
            second_half * cosine + first_half * sine_table,
        ],
        axis=-1,
    )


def project(source_rows, norm_gain, w_query, w_key, w_value):
    packed_weight = jnp.concatenate([w_query, w_key, w_value], axis=1)
    weight = lax.all_gather(packed_weight, "dp", axis=0, tiled=True)
    gathered = lax.all_gather(source_rows, "tensor", axis=1, tiled=True)
    widened = gathered.astype(jnp.float32)
    row_scale = lax.rsqrt(jnp.mean(widened * widened, axis=1, keepdims=True) + norm_eps)
    normed = (widened * row_scale * norm_gain).astype(jnp.bfloat16)
    return jnp.dot(normed, weight, preferred_element_type=jnp.float32)


def rotate_round(projected, token_positions, rotated_width, head_dim):
    total_rows = projected.shape[0]
    rotated = rotary_embedding(
        projected[:, :rotated_width].reshape(total_rows, -1, head_dim), token_positions
    ).reshape(total_rows, -1)
    return jnp.concatenate([rotated, projected[:, rotated_width:]], axis=1).astype(jnp.bfloat16)


def attend(packed, doc_lengths, query_width, key_width, head_dim, doc_max):
    total_rows = packed.shape[0]
    doc_total = total_rows // doc_max
    value_head_rows = key_width // head_dim
    heads_per_group = query_width // key_width
    queries = packed[:, :query_width].reshape(
        doc_total, doc_max, value_head_rows, heads_per_group, head_dim
    )
    key_rows = packed[:, query_width : query_width + key_width].reshape(
        doc_total, doc_max, value_head_rows, head_dim
    )
    value_rows = packed[:, query_width + key_width :].reshape(
        doc_total, doc_max, value_head_rows, head_dim
    )
    scores = jnp.einsum(
        "jqhgd,jkhd->jhgqk", queries, key_rows, preferred_element_type=jnp.float32
    ) / math.sqrt(head_dim)
    order_range = jnp.arange(doc_max)
    causal = order_range[:, None] >= order_range[None, :]
    scores = jnp.where(causal, scores, -jnp.inf)
    row_peak = jnp.max(scores, axis=-1, keepdims=True)
    exponent = jnp.exp(scores - row_peak)
    probability = (exponent / jnp.sum(exponent, axis=-1, keepdims=True)).astype(jnp.bfloat16)
    blended = jnp.einsum(
        "jhgqk,jkhd->jqhgd", probability, value_rows, preferred_element_type=jnp.float32
    )
    blended = blended.reshape(doc_total, doc_max, query_width)
    row_valid = order_range[None, :] < doc_lengths[:, None]
    result = jnp.where(row_valid[..., None], blended, 0.0)
    return result.reshape(total_rows, query_width).astype(jnp.bfloat16)


def local(
    activations, norm_gain, w_query, w_key, w_value, lengths, languages, lang_caps, dest_shard
):
    shard_count = lax.axis_size("dp")
    my_shard = lax.axis_index("dp")
    doc_count = lengths.shape[0]
    token_rows = activations.shape[0]
    rows_peer = token_rows // doc_count
    doc_max = rows_peer * shard_count
    docs_here = doc_count // shard_count
    head_dim = HEAD_WIDTH
    query_width = w_query.shape[1]
    key_width = w_key.shape[1]
    language_table = jnp.arange(lang_caps.shape[0])
    cap_of_doc = jnp.sum(
        jnp.where(languages[:, None] == language_table[None, :], lang_caps[None, :], 0), axis=1
    )
    capped = jnp.minimum(lengths, cap_of_doc)
    doc_order = jnp.arange(doc_count)
    same_dest = dest_shard[:, None] == dest_shard[None, :]
    doc_rank = jnp.sum(
        (same_dest & (doc_order[None, :] < doc_order[:, None])).astype(jnp.int32), axis=1
    )
    target_slot = dest_shard * docs_here + doc_rank
    holder = jnp.sum(
        jnp.where(doc_order[:, None] == target_slot[None, :], doc_order[None, :], 0), axis=1
    )
    mine = lax.dynamic_slice_in_dim(holder, my_shard * docs_here, docs_here)
    doc_lengths = jnp.take(capped, mine)
    holder_grid = jnp.transpose(holder.reshape(shard_count, docs_here))
    send_index = (
        holder_grid[:, None, :] * rows_peer + jnp.arange(rows_peer)[None, :, None]
    ).reshape(-1)
    token_positions = (my_shard + shard_count * (jnp.arange(token_rows) % rows_peer)).astype(
        jnp.float32
    )
    projected = project(activations, norm_gain, w_query, w_key, w_value)
    packed = rotate_round(projected, token_positions, query_width + key_width, head_dim)
    outgoing = jnp.take(packed, send_index, axis=0, mode="clip").reshape(
        docs_here, rows_peer, shard_count, -1
    )
    arrived = lax.all_to_all(outgoing, "dp", split_axis=2, concat_axis=2, tiled=True)
    moved_rows = arrived.reshape(docs_here * doc_max, -1)
    return attend(moved_rows, doc_lengths, query_width, key_width, head_dim, doc_max)


def solution(mesh):
    return jax.shard_map(
        local,
        mesh=mesh,
        in_specs=(
            P("dp", "tensor"),
            P(),
            P("dp", "tensor"),
            P("dp", "tensor"),
            P("dp", "tensor"),
            P(),
            P(),
            P(),
            P(),
        ),
        out_specs=P("dp", "tensor"),
        check_vma=False,
    )
```

profile of v0, /device:TPU:1, one launch (start us, length us, event | category | flops | bytes accessed | tf_op | source)
XLA Modules:
  0.0 293.0 jit_solution(14304292000981293359)
XLA Ops:
  6.5 0.7 all-gather.3.cloned.1.call-update
  7.3 1.7 pad_maximum_fusion.2
  9.1 0.2 convert_reduce_fusion
  9.3 0.1 select_reduce_fusion
  9.4 0.1 mul.133
  9.6 0.1 reshape.215
  9.7 0.5 multiply_cosine_fusion
  10.3 88.1 %all-gather.3.cloned.1.call-done = bf16[512,8192]{1,0:T(8,128)(2,1)} async-done(((bf16[512,2048]{1,0:T(8,128)(2,1)}), bf16[512,8192]{1,0:T(8,128)(2,1)}) %all-gather.3.cloned.1.call-update) | async-done | bytes 8388624 | tf_op jit(solution)/shard_map/all_gather | solution.py:33
  98.4 5.1 %fusion = f32[512]{0:T(512)S(1)} fusion(bf16[512,8192]{1,0:T(8,128)(2,1)} %all-gather.3.cloned.1.call-done), kind=kLoop, calls=%fused_computation.4 | loop fusion | flops 12582400 | bytes 8390656 | tf_op jit(solution)/shard_map/reduce_sum | solution.py:35
  103.5 109.2 %all-gather.5.cloned.1.call-done = bf16[8192,1280]{1,0:T(8,128)(2,1)} async-done(((bf16[128,1280]{1,0:T(8,128)(2,1)}), bf16[8192,1280]{1,0:T(8,128)(2,1)}) %all-gather.5.cloned.1.call-update) | async-done | bytes 20971536 | tf_op jit(solution)/shard_map/all_gather | solution.py:32
  212.7 16.5 %fusion.3 = f32[512,1280]{1,0:T(8,128)S(1)} fusion(bf16[8192,1280]{1,0:T(8,128)(2,1)} %all-gather.5.cloned.1.call-done, bf16[512,8192]{1,0:T(8,128)(2,1)} %all-gather.3.cloned.1.call-done, f32[8192]{0:T(1024)S(1)} %copy-done, f32[512]{0:T(512)S(1)} %add_rsqrt_fusion), kind=kOutput, calls=%fused_computation.7 | convolution fusion | flops 10754195456 | bytes 32016384 | tf_op jit(solution)/shard_map/dot_general | solution.py:37
  229.3 1.6 slice.33
  230.9 2.0 copy.28
  232.9 0.4 subtract_convert_fusion
  233.4 1.4 copy.29
  234.8 1.4 pad_maximum_fusion
  236.2 2.1 gather_fusion.1
  238.4 2.1 copy.31
  240.4 6.0 %all-to-all-start = ((bf16[2,4,64,1280]{3,1,0,2:T(4,128)(2,1)}), bf16[2,4,64,1280]{3,1,0,2:T(4,128)(2,1)S(1)}, u32[]{:S(2)}, u32[]{:S(2)}) async-start(bf16[2,4,64,1280]{3,1,0,2:T(4,128)(2,1)} %copy.31), calls=%async_computation | async-start | bytes 2621440 | tf_op jit(solution)/shard_map/all_to_all | solution.py:121
  246.4 0.1 select_reduce_fusion.1
  246.5 0.1 compare_select_fusion
  246.6 0.6 gather_fusion
  247.3 0.1 and_select_fusion
  247.5 33.1 %all-to-all-done = bf16[2,4,64,1280]{3,1,0,2:T(4,128)(2,1)S(1)} async-done(((bf16[2,4,64,1280]{3,1,0,2:T(4,128)(2,1)}), bf16[2,4,64,1280]{3,1,0,2:T(4,128)(2,1)S(1)}, u32[]{:S(2)}, u32[]{:S(2)}) %all-to-all-start) | async-done | bytes 1310752 | tf_op jit(solution)/shard_map/all_to_all | solution.py:121
  280.5 0.2 copy.32
  280.8 0.1 slice_bitcast_fusion
  280.9 0.3 copy.42
  281.2 0.8 fusion.8
  282.0 0.9 fusion.7
  282.9 1.3 fusion.13
  284.2 0.8 copy.36
  284.9 1.2 fusion.9
  (29 shorter events, 0.5 us)
Async XLA Ops:
  6.5 2.5 copy-start.1
  6.5 91.9 %all-gather.3.cloned.1.call-start = ((), (), s32[]{:S(2)}) async-start(), calls=%async_computation.1 | async-start | bytes 10485760 | tf_op jit(solution)/shard_map/all_gather | solution.py:33
  7.3 205.5 %all-gather.5.cloned.1.call-start = ((), (), s32[]{:S(2)}) async-start(), calls=%async_computation.2 | async-start | bytes 21299200 | tf_op jit(solution)/shard_map/all_gather | solution.py:32
  10.3 202.4 %copy-start = (f32[8192]{0:T(1024)S(1)}, f32[8192]{0:T(1024)}, u32[]{:S(2)}) copy-start(f32[8192]{0:T(1024)} %param.10) | copy-start | bytes 98308
  238.3 8.1 %copy-start.2 = (s32[30]{0:T(128)S(1)}, s32[30]{0:T(128)}, u32[]{:S(2)}) copy-start(s32[30]{0:T(128)} %param.16) | copy-start | bytes 364
  238.3 8.1 %copy-start.3 = (s32[128]{0:T(128)S(1)}, s32[128]{0:T(128)}, u32[]{:S(2)}) copy-start(s32[128]{0:T(128)} %param.15) | copy-start | bytes 1540
  238.3 8.2 %copy-start.4 = (s32[128]{0:T(128)S(1)}, s32[128]{0:T(128)}, u32[]{:S(2)}) copy-start(s32[128]{0:T(128)} %param.14) | copy-start | bytes 1540
  240.4 40.1 %all-to-all-start = ((bf16[2,4,64,1280]{3,1,0,2:T(4,128)(2,1)}), bf16[2,4,64,1280]{3,1,0,2:T(4,128)(2,1)S(1)}, u32[]{:S(2)}, u32[]{:S(2)}) async-start(bf16[2,4,64,1280]{3,1,0,2:T(4,128)(2,1)} %copy.31), calls=%async_computation | async-start | bytes 2621440 | tf_op jit(solution)/shard_map/all_to_all | solution.py:121
Sparse Core Ops, SparseCore 0:
  9.1 89.2 all-gather.2
  101.1 111.5 all-gather.4
where the time goes:
time: 293 us
  waiting for transfers between devices  231 us (79%)
  matrix products  18.6 us (6%)
  between operations  13.6 us (5%)
  other arithmetic  12 us (4%)
  local copies, waits for them, and re-layouts  11.6 us (4%)
  starting transfers between devices  6.01 us (2%)
    all_gather x1, waiting for transfers between devices, project(): weight = lax.all_gather(packed_weight, 'dp', axis=0, tiled=True)  109 us
    all_gather x1, waiting for transfers between devices, project(): gathered = lax.all_gather(source_rows, 'tensor', axis=1, tiled=True)  88.1 us
    all_to_all x1, waiting for transfers between devices, local(): lax.all_to_all(outgoing, 'dp', split_axis=2, concat_axis=2, tiled=True)  33.1 us
    dot_general x1, matrix products, project(): return jnp.dot(normed, weight, preferred_element_type=jnp.float32)  16.5 us
    all_to_all x1, starting transfers between devices, local(): lax.all_to_all(outgoing, 'dp', split_axis=2, concat_axis=2, tiled=True)  5.97 us
  transfers between devices with their start and end apart: 3, of which 3 were waited for; matrix products, arithmetic and copies ran while one was open for 3% of the time, Pallas kernels for 0%

commit v1 on v0

--- a/solution.py
+++ b/solution.py
@@ -7,6 +7,28 @@
 HEAD_WIDTH = 128
 rope_base = 500000.0
 norm_eps = 1e-05
+
+
+def in_order(blocks, dim):
+    shape = list(blocks.shape[1:])
+    shape[dim] *= blocks.shape[0]
+    return jnp.moveaxis(blocks, 0, dim).reshape(shape)
+
+
+def gather_around(x, axis, dim):
+    size = lax.axis_size(axis)
+    pairs = [(i, (i + 1) % size) for i in range(size)]
+    back = [(b, a) for a, b in pairs]
+    lower, upper = ([], [])
+    for hop in range(size - 1):
+        if hop % 2 == 0:
+            lower.append(lax.ppermute(lower[-1] if lower else x, axis, pairs))
+        else:
+            upper.append(lax.ppermute(upper[-1] if upper else x, axis, back))
+    parts = jnp.stack([*lower[::-1], x, *upper])
+    shift = lax.axis_index(axis) - len(lower)
+    parts = parts[(jnp.arange(size) - shift) % size]
+    return in_order(parts, dim)
 
 
 def rotary_embedding(vectors, token_positions):
@@ -30,7 +52,7 @@
 def project(source_rows, norm_gain, w_query, w_key, w_value):
     packed_weight = jnp.concatenate([w_query, w_key, w_value], axis=1)
     weight = lax.all_gather(packed_weight, "dp", axis=0, tiled=True)
-    gathered = lax.all_gather(source_rows, "tensor", axis=1, tiled=True)
+    gathered = gather_around(source_rows, "tensor", 1)
     widened = gathered.astype(jnp.float32)
     row_scale = lax.rsqrt(jnp.mean(widened * widened, axis=1, keepdims=True) + norm_eps)
     normed = (widened * row_scale * norm_gain).astype(jnp.bfloat16)

time: 293 us -> 252 us (0.86)
  waiting for transfers between devices: 231 us -> 119 us
  local copies, waits for them, and re-layouts: 11.6 us -> 41.5 us
  other arithmetic: 12 us -> 36.7 us
  starting transfers between devices: 6.01 us -> 21.4 us
    all_gather x1, waiting for transfers between devices: 109 us -> 0.01 us  [project(): weight = lax.all_gather(packed_weight, 'dp', axis=0, tiled=True)]
    all_gather x1 -> x0, waiting for transfers between devices: 88.1 us -> none  [project(): gathered = lax.all_gather(source_rows, 'tensor', axis=1, tiled=True)]
    ppermute x0 -> x3, waiting for transfers between devices: none -> 85.4 us  [the longest x2 85.4 us: gather_around(): lower.append(lax.ppermute(lower[-1] if lower else x, axis, pairs))]
    convert_element_type x0 -> x2, other arithmetic: none -> 20.8 us  [the longest x1 11.6 us: project(): widened = gathered.astype(jnp.float32)]
    convert_element_type x0 -> x1, local copies, waits for them, and re-layouts: none -> 16.4 us  [project(): widened = gathered.astype(jnp.float32)]
    gather x0 -> x3, local copies, waits for them, and re-layouts: none -> 14 us  [gather_around(): parts = parts[(jnp.arange(size) - shift) % size]]
    all_to_all x1, starting transfers between devices: 5.97 us -> 16.1 us  [local(): lax.all_to_all(outgoing, 'dp', split_axis=2, concat_axis=2, tiled=True)]
    ppermute x0 -> x3, starting transfers between devices: none -> 5.33 us  [the longest x2 3.97 us: gather_around(): lower.append(lax.ppermute(lower[-1] if lower else x, axis, pairs))]
  transfers between devices with their start and end apart: 3 -> 5, of which waited for: 3 -> 3; matrix products, arithmetic and copies ran while one was open for 3% -> 25% of each run, Pallas kernels for 0% -> 0%
where the time goes in v1:
time: 252 us; the launch traced here: 251 us
  waiting for transfers between devices  119 us (47%)
  local copies, waits for them, and re-layouts  41.5 us (16%)
  other arithmetic  36.7 us (15%)
  starting transfers between devices  21.4 us (8%)
  matrix products  19.1 us (8%)
  between operations  13.7 us (5%)
    ppermute x2, waiting for transfers between devices, gather_around(): lower.append(lax.ppermute(lower[-1] if lower else x, axis, pairs))  85.4 us
    all_to_all x1, waiting for transfers between devices, local(): lax.all_to_all(outgoing, 'dp', split_axis=2, concat_axis=2, tiled=True)  33.1 us
    dot_general x1, matrix products, project(): return jnp.dot(normed, weight, preferred_element_type=jnp.float32)  17 us
    convert_element_type x1, local copies, waits for them, and re-layouts, project(): widened = gathered.astype(jnp.float32)  16.4 us
    all_to_all x1, starting transfers between devices, local(): lax.all_to_all(outgoing, 'dp', split_axis=2, concat_axis=2, tiled=True)  16.1 us
    gather x3, local copies, waits for them, and re-layouts, gather_around(): parts = parts[(jnp.arange(size) - shift) % size]  14 us
    convert_element_type x1, other arithmetic, project(): widened = gathered.astype(jnp.float32)  11.6 us
    convert_element_type x1, other arithmetic, project(): normed = (widened * row_scale * norm_gain).astype(jnp.bfloat16)  9.25 us
  transfers between devices with their start and end apart: 5, of which 3 were waited for; matrix products, arithmetic and copies ran while one was open for 25% of the time, Pallas kernels for 0%

profile of v1, /device:TPU:1, one launch (start us, length us, event | category | flops | bytes accessed | tf_op | source)
XLA Modules:
  0.0 250.9 jit_solution(5960612333627656045)
XLA Ops:
  6.5 1.7 pad_maximum_fusion.4
  8.3 2.1 collective-permute-start
  10.4 1.4 collective-permute-start.2
  11.8 43.4 %collective-permute-done = bf16[512,2048]{1,0:T(8,128)(2,1)S(1)} collective-permute-done((bf16[512,2048]{1,0:T(8,128)(2,1)}, bf16[512,2048]{1,0:T(8,128)(2,1)S(1)}, u32[]{:S(2)}, u32[]{:S(2)}) %collective-permute-start) | collective-permute-done | bytes 2097184 | tf_op jit(solution)/shard_map/ppermute | solution.py:25
  55.1 1.9 collective-permute-start.1
  57.0 0.9 convert_reduce_fusion
  57.9 0.7 multiply_add_fusion
  59.1 0.5 multiply_cosine_fusion
  59.6 42.0 %collective-permute-done.1 = bf16[512,2048]{1,0:T(8,128)(2,1)} collective-permute-done((bf16[512,2048]{1,0:T(8,128)(2,1)S(1)}, bf16[512,2048]{1,0:T(8,128)(2,1)}, u32[]{:S(2)}, u32[]{:S(2)}) %collective-permute-start.1) | collective-permute-done | bytes 2097184 | tf_op jit(solution)/shard_map/ppermute | solution.py:25
  101.7 4.0 %pad_maximum_fusion = bf16[4,512,2048]{2,1,0:T(8,128)(2,1)S(1)} fusion(bf16[1,512,2048]{2,1,0:T(8,128)(2,1)} %bitcast.3, bf16[1,512,2048]{2,1,0:T(8,128)(2,1)} %bitcast.75, bf16[1,512,2048]{2,1,0:T(8,128)(2,1)S(1)} %bitcast.76, bf16[1,512,2048]{2,1,0:T(8,128)(2,1)} %bitcast), kind=kLoop, calls=%fused_computation.10 | loop fusion | flops 12582912 | bytes 16777216 | tf_op jit(solution)/shard_map/stack | solution.py:28
  105.7 3.9 %fusion.25 = (bf16[4,512,1024]{2,1,0:T(8,128)(2,1)}, bf16[4,512,1024]{2,1,0:T(8,128)(2,1)}) fusion(bf16[4,512,2048]{2,1,0:T(8,128)(2,1)S(1)} %pad_maximum_fusion), kind=kLoop, calls=%fused_computation.69 | loop fusion | bytes 16777216 | tf_op jit(solution)/shard_map/gather | solution.py:30
  109.6 5.1 %gather_fusion.2 = bf16[4,512,1024]{2,1,0:T(8,128)(2,1)} fusion(bf16[4,512,1024]{2,1,0:T(8,128)(2,1)} %get-tuple-element.5, s32[1024]{0:T(1024)S(1)} %pad_clamp_fusion.1), kind=kCustom, calls=%fused_computation.2 | custom fusion | bytes 8388624 | tf_op jit(solution)/shard_map/gather | solution.py:30
  114.7 5.1 %gather_fusion.3 = bf16[4,512,1024]{2,1,0:T(8,128)(2,1)} fusion(bf16[4,512,1024]{2,1,0:T(8,128)(2,1)} %get-tuple-element.6, s32[1024]{0:T(1024)S(1)} %pad_clamp_fusion.1), kind=kCustom, calls=%fused_computation.3 | custom fusion | bytes 8388624 | tf_op jit(solution)/shard_map/gather | solution.py:30
  119.7 11.6 %convert_bitcast_fusion = f32[512,4,2048]{2,0,1:T(8,128)} fusion(bf16[4,512,1024]{2,1,0:T(8,128)(2,1)} %gather_fusion.3, bf16[4,512,1024]{2,1,0:T(8,128)(2,1)} %gather_fusion.2), kind=kLoop, calls=%fused_computation.5 | loop fusion | flops 16777216 | bytes 25165824 | tf_op jit(solution)/shard_map/convert_element_type | solution.py:56
  131.3 16.4 %copy.37 = f32[512,4,2048]{0,2,1:T(8,128)} copy(f32[512,4,2048]{2,0,1:T(8,128)} %convert_bitcast_fusion) | data formatting | bytes 33554432 | tf_op jit(solution)/shard_map/convert_element_type | solution.py:56
  147.6 4.9 %fusion = f32[512]{0:T(512)S(1)} fusion(bf16[4,512,1024]{2,1,0:T(8,128)(2,1)} %gather_fusion.3, bf16[4,512,1024]{2,1,0:T(8,128)(2,1)} %gather_fusion.2), kind=kLoop, calls=%fused_computation.6 | loop fusion | flops 25165312 | bytes 8390656 | tf_op jit(solution)/shard_map/reduce_sum | solution.py:57
  152.5 9.3 %fusion.2 = bf16[512,8192]{0,1:T(8,128)(2,1)} fusion(f32[512,4,2048]{0,2,1:T(8,128)} %copy.37, f32[8192]{0:T(1024)S(1)} %copy-done, f32[512]{0:T(512)S(1)} %add_rsqrt_fusion), kind=kLoop, calls=%fused_computation.9 | loop fusion | flops 12582912 | bytes 25200640 | tf_op jit(solution)/shard_map/convert_element_type | solution.py:58
  161.8 17.0 %fusion.27 = f32[512,1280]{1,0:T(8,128)S(1)} fusion(bf16[512,8192]{0,1:T(8,128)(2,1)} %fusion.2, bf16[8192,1280]{1,0:T(8,128)(2,1)} %all-gather.2.cloned.1.call-done), kind=kOutput, calls=%fused_computation.71 | convolution fusion | flops 10737418240 | bytes 31981568 | tf_op jit(solution)/shard_map/dot_general | solution.py:59
  178.8 1.6 slice.37
  180.4 2.0 copy.38
  182.4 0.4 subtract_convert_fusion
  182.9 0.7 copy.39
  183.8 2.4 gather_fusion.1
  186.2 2.1 copy.41
  188.2 16.1 %all-to-all-start = ((bf16[2,4,64,1280]{3,1,0,2:T(4,128)(2,1)}), bf16[2,4,64,1280]{3,1,0,2:T(4,128)(2,1)S(1)}, u32[]{:S(2)}, u32[]{:S(2)}) async-start(bf16[2,4,64,1280]{3,1,0,2:T(4,128)(2,1)} %copy.41), calls=%async_computation | async-start | bytes 2621440 | tf_op jit(solution)/shard_map/all_to_all | solution.py:143
  204.5 0.6 gather_fusion
  205.4 33.1 %all-to-all-done = bf16[2,4,64,1280]{3,1,0,2:T(4,128)(2,1)S(1)} async-done(((bf16[2,4,64,1280]{3,1,0,2:T(4,128)(2,1)}), bf16[2,4,64,1280]{3,1,0,2:T(4,128)(2,1)S(1)}, u32[]{:S(2)}, u32[]{:S(2)}) %all-to-all-start) | async-done | bytes 1310752 | tf_op jit(solution)/shard_map/all_to_all | solution.py:143
  239.1 0.8 fusion.4
  239.9 0.9 fusion.3
  240.8 1.3 fusion.9
  242.1 0.8 copy.46
  242.9 1.2 fusion.5
  (39 shorter events, 1.7 us)
Async XLA Ops:
  6.5 155.3 %all-gather.2.cloned.1.call-start = ((), (), s32[]{:S(2)}) async-start(), calls=%async_computation.1 | async-start | bytes 21299200 | tf_op jit(solution)/shard_map/all_gather | solution.py:54
  8.3 46.8 %collective-permute-start = (bf16[512,2048]{1,0:T(8,128)(2,1)}, bf16[512,2048]{1,0:T(8,128)(2,1)S(1)}, u32[]{:S(2)}, u32[]{:S(2)}) collective-permute-start(bf16[512,2048]{1,0:T(8,128)(2,1)} %param.9), channel_id=1, source_target_pairs={{0,1},{1,2},{2,3},{3,0},{4,5},{5,6},{6,7},{7,4},{8,9},{9,10},{10,1... | collective-permute-start | bytes 6291464 | tf_op jit(solution)/shard_map/ppermute | solution.py:25
  10.4 49.2 %collective-permute-start.2 = (bf16[512,2048]{1,0:T(8,128)(2,1)}, bf16[512,2048]{1,0:T(8,128)(2,1)}, u32[]{:S(2)}, u32[]{:S(2)}) collective-permute-start(bf16[512,2048]{1,0:T(8,128)(2,1)} %param.9), channel_id=1, source_target_pairs={{1,0},{2,1},{3,2},{0,3},{5,4},{6,5},{7,6},{4,7},{9,8},{10,9},{11,1... | collective-permute-start | bytes 6291464 | tf_op jit(solution)/shard_map/ppermute | solution.py:27
  55.1 46.5 %collective-permute-start.1 = (bf16[512,2048]{1,0:T(8,128)(2,1)S(1)}, bf16[512,2048]{1,0:T(8,128)(2,1)}, u32[]{:S(2)}, u32[]{:S(2)}) collective-permute-start(bf16[512,2048]{1,0:T(8,128)(2,1)S(1)} %collective-permute-done), channel_id=1, source_target_pairs={{0,1},{1,2},{2,3},{3,0},{4,5},{5,6},{6,7},{7,4},{8,9},{9,10},{10,1... | collective-permute-start | bytes 6291464 | tf_op jit(solution)/shard_map/ppermute | solution.py:25
  147.6 4.9 %copy-start = (f32[8192]{0:T(1024)S(1)}, f32[8192]{0:T(1024)}, u32[]{:S(2)}) copy-start(f32[8192]{0:T(1024)} %param.10) | copy-start | bytes 98308
  186.1 18.2 %copy-start.1 = (s32[30]{0:T(128)S(1)}, s32[30]{0:T(128)}, u32[]{:S(2)}) copy-start(s32[30]{0:T(128)} %param.16) | copy-start | bytes 364
  186.1 18.2 %copy-start.2 = (s32[128]{0:T(128)S(1)}, s32[128]{0:T(128)}, u32[]{:S(2)}) copy-start(s32[128]{0:T(128)} %param.15) | copy-start | bytes 1540
  186.1 18.3 %copy-start.3 = (s32[128]{0:T(128)S(1)}, s32[128]{0:T(128)}, u32[]{:S(2)}) copy-start(s32[128]{0:T(128)} %param.14) | copy-start | bytes 1540
  188.2 50.2 %all-to-all-start = ((bf16[2,4,64,1280]{3,1,0,2:T(4,128)(2,1)}), bf16[2,4,64,1280]{3,1,0,2:T(4,128)(2,1)S(1)}, u32[]{:S(2)}, u32[]{:S(2)}) async-start(bf16[2,4,64,1280]{3,1,0,2:T(4,128)(2,1)} %copy.41), calls=%async_computation | async-start | bytes 2621440 | tf_op jit(solution)/shard_map/all_to_all | solution.py:143
Sparse Core Ops, SparseCore 0:
  10.1 114.1 all-gather.1
